TPU v7x, 32 devices: a whole 2x2x4 slice. The times are simulated.
32 devices in a mesh: dom: 16 (over z, y, x), band: 2 (over core).
Axes of the slice: x: 2, y: 2, z: 4, core: 2. Of those that a mesh axis runs over, the one named last changes fastest.
Arguments:
- wavefunctions: bfloat16 [32768, 1024], P('dom', 'band'), may hold values from -4 to 4
- mass_scale: float32 [32768], P('dom'), may hold values from 0.7 to 1.4
- cell_matrices: bfloat16 [128, 512, 512], P('dom')
- connectivity: int32 [128, 512], P('dom'), may hold values from 0 to 2303, as said below
- face_index: int32 [4096], P('dom'), may hold values from 0 to 2047, as said below
Outputs:
- rotated: float32 [32768, 1024], P('dom', 'band')
Inputs may be any that keep to these rules, and one draw needn't show every extreme that they name: `connectivity`: local numbers of each cell's 512 nodes within its domain: below 2048 the domain's own nodes, from 2048 on the entries of the next domain's face list in order; every local number appears in its domain, and a number may repeat. `face_index`: local numbers of 256 own nodes of each domain, in the order that the previous domain uses; a number may repeat.
All inputs are finite; a program needn't handle non-finite values.
Results may differ from a plain program's by a relative error of at most 0.011.
Values may be sent and summed in bfloat16 or wider, within the bound.
A program may use at most 64 MiB of HBM per device.

v0:
```python
import jax
import jax.numpy as jnp
from jax import lax
from jax.sharding import PartitionSpec as P

STATES = 1024
DEGREE = 3
NS_ITERS = 2


filter_center = 5.0
filter_half = 5.0


def passed_along(value, axis, steps):
    count = lax.axis_size(axis)
    initial, last = (max(0, -steps), min(count, count - steps))
    return lax.ppermute(value, axis, [(source, source + steps) for source in range(initial, last)])


def apply_hamiltonian(vectors, mass_scale, cell_matrices, connectivity, face_index):
    own_nodes, band_width = vectors.shape
    scaled = (mass_scale[:, None] * vectors).astype(jnp.bfloat16)
    face_rows = jnp.take(scaled, face_index, axis=0)
    received = passed_along(face_rows, "dom", -1)
    extended = jnp.concatenate([scaled, received], axis=0)
    gathered = jnp.take(extended, connectivity, axis=0)
    products = jnp.einsum(
        "cij,cjs->cis", cell_matrices, gathered, preferred_element_type=jnp.float32
    )
    assembled = jnp.zeros((extended.shape[0], band_width), jnp.float32)
    assembled = assembled.at[connectivity.reshape(-1)].add(products.reshape(-1, band_width))
    returned = passed_along(assembled[own_nodes:], "dom", 1)
    summed = assembled[:own_nodes].at[face_index].add(returned)
    return mass_scale[:, None] * summed


def on_device(wavefunctions, mass_scale, cell_matrices, connectivity, face_index):
    highest = lax.Precision.HIGHEST

    def hamiltonian(vectors):
        return apply_hamiltonian(vectors, mass_scale, cell_matrices, connectivity, face_index)

    previous = wavefunctions.astype(jnp.float32)
    current = (hamiltonian(previous) - filter_center * previous) / filter_half
    for sweep_index in range(DEGREE - 1):
        following = 2.0 * (hamiltonian(current) - filter_center * current) / filter_half - previous
        previous, current = (current, following)
    own_nodes, band_width = current.shape
    rounded = current.astype(jnp.bfloat16)
    contract_rows = (((0,), (0,)), ((), ()))
    partial_margin = lax.dot_general(
        lax.all_gather(rounded, "band", axis=1, tiled=True),
        rounded,
        contract_rows,
        preferred_element_type=jnp.float32,
    )
    domains = lax.axis_size("dom")
    tile_rows = STATES // domains
    dom_position = lax.axis_index("dom")
    margin_tile = lax.psum_scatter(partial_margin, "dom", scatter_dimension=0, tiled=True)
    margin_tile = margin_tile / (own_nodes * domains)
    row_ids = dom_position * tile_rows + lax.broadcasted_iota(jnp.int32, (tile_rows, band_width), 0)
    col_ids = lax.axis_index("band") * band_width + lax.broadcasted_iota(
        jnp.int32, (tile_rows, band_width), 1
    )
    identity = (row_ids == col_ids).astype(jnp.float32)
    trace_part = jnp.sum(margin_tile * identity)
    mean_eigen = lax.psum(trace_part, ("dom", "band")) / STATES
    current_y = margin_tile / mean_eigen
    current_z = identity
    for ns_index in range(NS_ITERS):
        z_panel, y_panel = (
            lax.all_gather(current_z.astype(jnp.bfloat16), "band", axis=1, tiled=True).astype(
                current_z.dtype
            ),
            lax.all_gather(current_y.astype(jnp.bfloat16), "band", axis=1, tiled=True).astype(
                current_y.dtype
            ),
        )
        product = jnp.dot(
            z_panel,
            lax.all_gather(current_y, "dom", axis=0, tiled=True),
            precision=highest,
            preferred_element_type=jnp.float32,
        )
        correction = 1.5 * identity - 0.5 * product
        segment = lax.all_gather(correction, "dom", axis=0, tiled=True)
        new_y = jnp.dot(y_panel, segment, precision=highest, preferred_element_type=jnp.float32)
        new_z = jnp.dot(z_panel, segment, precision=highest, preferred_element_type=jnp.float32)
        current_y = new_y
        current_z = new_z
    inverse_root = current_z / jnp.sqrt(mean_eigen)
    root_columns = lax.all_gather(inverse_root, "dom", axis=0, tiled=True)
    return jnp.dot(
        lax.all_gather(current, "band", axis=1, tiled=True),
        root_columns,
        precision=highest,
        preferred_element_type=jnp.float32,
    )


def solution(mesh):
    return jax.shard_map(
        on_device,
        mesh=mesh,
        in_specs=(P("dom", "band"), P("dom"), P("dom", None, None), P("dom", None), P("dom")),
        out_specs=P("dom", "band"),
        check_vma=False,
    )
```

profile of v0, /device:TPU:0, one launch (start us, length us, event | category | flops | bytes accessed | tf_op | source)
XLA Modules:
  0.0 798.3 jit_solution(13273846610441065336)
XLA Ops:
  7.9 2.0 fusion
  12.7 9.7 %collective-permute-done = bf16[256,512]{1,0:T(8,128)(2,1)S(1)} collective-permute-done((bf16[256,512]{1,0:T(8,128)(2,1)S(1)}, bf16[256,512]{1,0:T(8,128)(2,1)S(1)}, u32[]{:S(2)}, u32[]{:S(2)}) %collective-permute-start) | collective-permute-done | bytes 262176 | tf_op jit(solution)/shard_map/ppermute | solution.py:18
  24.2 17.3 %gather_fusion.1 = bf16[4096,512]{1,0:T(8,128)(2,1)} fusion(bf16[2304,512]{1,0:T(8,128)(2,1)S(1)} %pad_maximum_fusion, s32[4096]{0:T(1024)S(1)} %broadcast_clamp_fusion), kind=kCustom, calls=%fused_computation.1.clone | custom fusion | bytes 8404992 | tf_op jit(solution)/shard_map/jit(_take)/gather | solution.py:27
  41.5 9.1 %fusion.6 = f32[8,512,512]{1,2,0:T(8,128)} fusion(bf16[8,512,512]{2,1,0:T(8,128)(2,1)} %param.11, bf16[8,512,512]{2,1,0:T(8,128)(2,1)} %bitcast.38, pred[8,512]{1,0:T(8,128)(4,1)S(1)} %compare_and_fusion), kind=kOutput, calls=%fused_computation.21 | convolution fusion | flops 2149580800 | bytes 16781312 | tf_op jit(solution)/shard_map/cij,cjs->cis/dot_general | solution.py:28
  50.6 27.6 %scatter_custom_fusion = f32[2304,512]{1,0:T(8,128)} fusion(s32[4096]{0:T(1024)S(1)} %bitcast.46, f32[4096,512]{1,0:T(8,128)} %bitcast.41, f32[]{:T(128)} %constant.31.clone.1), kind=kCustom, calls=%fused_computation.36 | custom fusion | flops 2097152 | bytes 4719104 | tf_op jit(solution)/shard_map/scatter-add | solution.py:32
  79.3 4.6 collective-permute-start.1
  83.9 4.7 slice.36
  88.6 5.6 collective-permute-done.1
  94.2 6.2 scatter_fusion
  100.4 3.6 multiply_convert_fusion.1
  104.1 3.1 gather_fusion.2
  108.7 7.5 collective-permute-done.2
  118.0 17.3 %gather_fusion.3 = bf16[4096,512]{1,0:T(8,128)(2,1)} fusion(bf16[2304,512]{1,0:T(8,128)(2,1)S(1)} %pad_maximum_fusion.1, s32[4096]{0:T(1024)S(1)} %broadcast_clamp_fusion), kind=kCustom, calls=%fused_computation.4.clone | custom fusion | bytes 8404992 | tf_op jit(solution)/shard_map/jit(_take)/gather | solution.py:27
  135.3 9.1 %fusion.4 = f32[8,512,512]{1,2,0:T(8,128)} fusion(bf16[8,512,512]{2,1,0:T(8,128)(2,1)} %param.11, bf16[8,512,512]{2,1,0:T(8,128)(2,1)} %bitcast.39, pred[8,512]{1,0:T(8,128)(4,1)S(1)} %compare_and_fusion), kind=kOutput, calls=%fused_computation.19 | convolution fusion | flops 2149580800 | bytes 16781312 | tf_op jit(solution)/shard_map/cij,cjs->cis/dot_general | solution.py:28
  144.4 27.6 %scatter_custom_fusion.2 = f32[2304,512]{1,0:T(8,128)} fusion(s32[4096]{0:T(1024)S(1)} %bitcast.47, f32[4096,512]{1,0:T(8,128)} %bitcast.42, f32[]{:T(128)} %constant.31.clone.1), kind=kCustom, calls=%fused_computation.34 | custom fusion | flops 2097152 | bytes 4719104 | tf_op jit(solution)/shard_map/scatter-add | solution.py:32
  173.1 4.6 collective-permute-start.3
  177.7 4.6 slice.38
  182.3 3.7 collective-permute-done.3
  186.0 6.1 scatter_fusion.1
  192.1 5.2 multiply_convert_fusion
  197.3 3.1 gather_fusion.4
  202.0 7.2 collective-permute-done.4
  211.0 17.3 %gather_fusion.5 = bf16[4096,512]{1,0:T(8,128)(2,1)} fusion(bf16[2304,512]{1,0:T(8,128)(2,1)S(1)} %pad_maximum_fusion.2, s32[4096]{0:T(1024)S(1)} %broadcast_clamp_fusion), kind=kCustom, calls=%fused_computation.5.clone | custom fusion | bytes 8404992 | tf_op jit(solution)/shard_map/jit(_take)/gather | solution.py:27
  228.3 9.1 %fusion.2 = f32[8,512,512]{1,2,0:T(8,128)} fusion(bf16[8,512,512]{2,1,0:T(8,128)(2,1)} %param.11, bf16[8,512,512]{2,1,0:T(8,128)(2,1)} %bitcast.37, pred[8,512]{1,0:T(8,128)(4,1)S(1)} %compare_and_fusion), kind=kOutput, calls=%fused_computation.17 | convolution fusion | flops 2149580800 | bytes 16781312 | tf_op jit(solution)/shard_map/cij,cjs->cis/dot_general | solution.py:28
  237.4 27.6 %scatter_custom_fusion.4 = f32[2304,512]{1,0:T(8,128)} fusion(s32[4096]{0:T(1024)S(1)} %bitcast.48, f32[4096,512]{1,0:T(8,128)} %bitcast.40, f32[]{:T(128)} %constant.31.clone.1), kind=kCustom, calls=%fused_computation.32 | custom fusion | flops 2097152 | bytes 4719104 | tf_op jit(solution)/shard_map/scatter-add | solution.py:32
  266.1 4.8 collective-permute-start.5
  271.0 4.6 slice.40
  275.6 2.3 collective-permute-done.5
  277.8 6.2 scatter_fusion.2
  284.0 7.4 fusion.29
  291.5 18.2 %all-gather.10.cloned.1.call-done = bf16[2048,1024]{1,0:T(8,128)(2,1)} async-done(((bf16[2048,512]{1,0:T(8,128)(2,1)}), bf16[2048,1024]{1,0:T(8,128)(2,1)}) %all-gather.10.cloned.1.call-update) | async-done | bytes 4194320 | tf_op jit(solution)/shard_map/all_gather | solution.py:53
  309.7 6.6 fusion.30
  316.4 82.7 %reduce-scatter.2.cloned.1.call-done = f32[64,512]{1,0:T(8,128)} async-done(((f32[1024,512]{1,0:T(8,128)}), f32[64,512]{1,0:T(8,128)}) %reduce-scatter.2.cloned.1.call-update) | async-done | bytes 131088 | tf_op jit(solution)/shard_map/reduce_scatter | solution.py:61
  400.8 37.0 %psum.7 = f32[]{:T(128)} all-reduce(f32[]{:T(128)} %fusion.23), channel_id=1, replica_groups=mesh['dom'=16,'band'=2] {'dom','band'}, use_global_device_ids=true, to_apply=%region_8.11 | all-reduce | flops 1 | bytes 8 | tf_op jit(solution)/shard_map/psum | solution.py:69
  440.5 1.9 all_gather.31
  442.4 58.9 %all-gather.12.cloned.1.call-done = f32[1024,512]{1,0:T(8,128)} async-done(((f32[64,512]{1,0:T(8,128)}), f32[1024,512]{1,0:T(8,128)}) %all-gather.12.cloned.1.call-update) | async-done | bytes 2097168 | tf_op jit(solution)/shard_map/all_gather | solution.py:83
  501.4 3.1 fusion.21
  504.6 1.9 all_gather.36
  506.5 57.4 %all-gather.14.cloned.1.call-done = f32[1024,512]{1,0:T(8,128)} async-done(((f32[64,512]{1,0:T(8,128)}), f32[1024,512]{1,0:T(8,128)}) %all-gather.14.cloned.1.call-update) | async-done | bytes 2097168 | tf_op jit(solution)/shard_map/all_gather | solution.py:88
  563.9 3.1 fusion.31
  567.1 2.5 convolution_convert_fusion
  571.4 54.9 %all-gather.16.cloned.1.call-done = f32[1024,512]{1,0:T(8,128)} async-done(((f32[64,512]{1,0:T(8,128)}), f32[1024,512]{1,0:T(8,128)}) %all-gather.16.cloned.1.call-update) | async-done | bytes 2097168 | tf_op jit(solution)/shard_map/all_gather | solution.py:83
  626.3 3.1 fusion.20
  630.4 58.5 %all-gather.18.cloned.1.call-done = f32[1024,512]{1,0:T(8,128)} async-done(((f32[64,512]{1,0:T(8,128)}), f32[1024,512]{1,0:T(8,128)}) %all-gather.18.cloned.1.call-update) | async-done | bytes 2097168 | tf_op jit(solution)/shard_map/all_gather | solution.py:88
  688.8 3.1 convolution_divide_fusion
  692.0 17.1 %all-gather.8.cloned.1.call-done = f32[2048,1024]{1,0:T(8,128)} async-done(((f32[2048,512]{1,0:T(8,128)}), f32[2048,1024]{1,0:T(8,128)}) %all-gather.8.cloned.1.call-update) | async-done | bytes 8388624 | tf_op jit(solution)/shard_map/all_gather | solution.py:96
  709.1 64.4 %all-gather.20.cloned.1.call-done = f32[1024,512]{1,0:T(8,128)} async-done(((f32[64,512]{1,0:T(8,128)}), f32[1024,512]{1,0:T(8,128)}) %all-gather.20.cloned.1.call-update) | async-done | bytes 2097168 | tf_op jit(solution)/shard_map/all_gather | solution.py:94
  773.4 17.6 %fusion.32 = f32[2048,512]{1,0:T(8,128)} fusion(f32[2048,1024]{1,0:T(8,128)} %all-gather.8.cloned.1.call-done, f32[1024,512]{1,0:T(8,128)} %all-gather.20.cloned.1.call-done), kind=kOutput, calls=%fused_computation.74 | convolution fusion | flops 12884901888 | bytes 14680064 | tf_op jit(solution)/shard_map/dot_general | solution.py:95
  (57 shorter events, 22.3 us)
Async XLA Ops:
  6.5 6.0 copy-start.5
  6.5 303.2 %all-gather.10.cloned.1.call-start = ((), (), s32[]{:S(2)}) async-start(), calls=%async_computation.2 | async-start | bytes 6291456 | tf_op jit(solution)/shard_map/all_gather | solution.py:53
  10.0 2.7 copy-start.3
  11.3 11.2 %collective-permute-start = (bf16[256,512]{1,0:T(8,128)(2,1)S(1)}, bf16[256,512]{1,0:T(8,128)(2,1)S(1)}, u32[]{:S(2)}, u32[]{:S(2)}) collective-permute-start(bf16[256,512]{1,0:T(8,128)(2,1)S(1)} %broadcast_select_fusion.2), channel_id=1, source_target_pairs={{2,0},{4,2},{6,4},{8,6},{10,8},{12,10},{14,12},{16,14},{18,16},{20... | collective-permute-start | bytes 786440 | tf_op jit(solution)/shard_map/ppermute | solution.py:18
  50.6 33.3 %copy-start.4 = (f32[2048]{0:T(1024)S(1)}, f32[2048]{0:T(1024)}, u32[]{:S(2)}) copy-start(f32[2048]{0:T(1024)} %param.10) | copy-start | bytes 24580
  79.3 14.9 %collective-permute-start.1 = (f32[256,512]{1,0:T(8,128)S(1)}, f32[256,512]{1,0:T(8,128)S(1)}, u32[]{:S(2)}, u32[]{:S(2)}) collective-permute-start(f32[256,512]{1,0:T(8,128)S(1)} %slice.37), channel_id=1, source_target_pairs={{0,2},{2,4},{4,6},{6,8},{8,10},{10,12},{12,14},{14,16},{16,18},{18... | collective-permute-start | bytes 1572872 | tf_op jit(solution)/shard_map/ppermute | solution.py:18
  88.6 11.8 %copy-start = (bf16[2048,512]{1,0:T(8,128)(2,1)S(1)}, bf16[2048,512]{1,0:T(8,128)(2,1)}, u32[]{:S(2)}) copy-start(bf16[2048,512]{1,0:T(8,128)(2,1)} %param.9) | copy-start | bytes 6291460
  107.3 9.0 %collective-permute-start.2 = (bf16[256,512]{1,0:T(8,128)(2,1)S(1)}, bf16[256,512]{1,0:T(8,128)(2,1)S(1)}, u32[]{:S(2)}, u32[]{:S(2)}) collective-permute-start(bf16[256,512]{1,0:T(8,128)(2,1)S(1)} %broadcast_select_fusion.1), channel_id=1, source_target_pairs={{2,0},{4,2},{6,4},{8,6},{10,8},{12,10},{14,12},{16,14},{18,16},{20... | collective-permute-start | bytes 786440 | tf_op jit(solution)/shard_map/ppermute | solution.py:18
  173.1 12.9 %collective-permute-start.3 = (f32[256,512]{1,0:T(8,128)S(1)}, f32[256,512]{1,0:T(8,128)S(1)}, u32[]{:S(2)}, u32[]{:S(2)}) collective-permute-start(f32[256,512]{1,0:T(8,128)S(1)} %slice.39), channel_id=1, source_target_pairs={{0,2},{2,4},{4,6},{6,8},{8,10},{10,12},{12,14},{14,16},{16,18},{18... | collective-permute-start | bytes 1572872 | tf_op jit(solution)/shard_map/ppermute | solution.py:18
  182.3 9.8 %copy-start.1 = (bf16[2048,512]{1,0:T(8,128)(2,1)S(1)}, bf16[2048,512]{1,0:T(8,128)(2,1)}, u32[]{:S(2)}) copy-start(bf16[2048,512]{1,0:T(8,128)(2,1)} %param.9) | copy-start | bytes 6291460
  200.5 8.7 %collective-permute-start.4 = (bf16[256,512]{1,0:T(8,128)(2,1)S(1)}, bf16[256,512]{1,0:T(8,128)(2,1)S(1)}, u32[]{:S(2)}, u32[]{:S(2)}) collective-permute-start(bf16[256,512]{1,0:T(8,128)(2,1)S(1)} %broadcast_select_fusion), channel_id=1, source_target_pairs={{2,0},{4,2},{6,4},{8,6},{10,8},{12,10},{14,12},{16,14},{18,16},{20... | collective-permute-start | bytes 786440 | tf_op jit(solution)/shard_map/ppermute | solution.py:18
  266.1 11.7 %collective-permute-start.5 = (f32[256,512]{1,0:T(8,128)S(1)}, f32[256,512]{1,0:T(8,128)S(1)}, u32[]{:S(2)}, u32[]{:S(2)}) collective-permute-start(f32[256,512]{1,0:T(8,128)S(1)} %slice.41), channel_id=1, source_target_pairs={{0,2},{2,4},{4,6},{6,8},{8,10},{10,12},{12,14},{14,16},{16,18},{18... | collective-permute-start | bytes 1572872 | tf_op jit(solution)/shard_map/ppermute | solution.py:18
  275.6 8.4 %copy-start.2 = (bf16[2048,512]{1,0:T(8,128)(2,1)S(1)}, bf16[2048,512]{1,0:T(8,128)(2,1)}, u32[]{:S(2)}) copy-start(bf16[2048,512]{1,0:T(8,128)(2,1)} %param.9) | copy-start | bytes 6291460
  291.4 107.7 %reduce-scatter.2.cloned.1.call-start = ((), (), s32[]{:S(2)}) async-start(), calls=%async_computation.3 | async-start | bytes 2228224 | tf_op jit(solution)/shard_map/reduce_scatter | solution.py:61
  316.3 185.1 %all-gather.12.cloned.1.call-start = ((), (), s32[]{:S(2)}) async-start(), calls=%async_computation.4 | async-start | bytes 2228224 | tf_op jit(solution)/shard_map/all_gather | solution.py:83
  440.1 123.7 %all-gather.14.cloned.1.call-start = ((), (), s32[]{:S(2)}) async-start(), calls=%async_computation.5 | async-start | bytes 2228224 | tf_op jit(solution)/shard_map/all_gather | solution.py:88
  504.5 121.8 %all-gather.16.cloned.1.call-start = ((), (), s32[]{:S(2)}) async-start(), calls=%async_computation.6 | async-start | bytes 2228224 | tf_op jit(solution)/shard_map/all_gather | solution.py:83
  567.0 121.8 %all-gather.18.cloned.1.call-start = ((), (), s32[]{:S(2)}) async-start(), calls=%async_computation.7 | async-start | bytes 2228224 | tf_op jit(solution)/shard_map/all_gather | solution.py:88
  629.5 79.6 %all-gather.8.cloned.1.call-start = ((), (), s32[]{:S(2)}) async-start(), calls=%async_computation.1 | async-start | bytes 12582912 | tf_op jit(solution)/shard_map/all_gather | solution.py:96
  630.3 143.2 %all-gather.20.cloned.1.call-start = ((), (), s32[]{:S(2)}) async-start(), calls=%async_computation.8 | async-start | bytes 2228224 | tf_op jit(solution)/shard_map/all_gather | solution.py:94
Sparse Core Ops, SparseCore 0:
  291.5 18.1 all-gather.9
  316.4 82.6 reduce-scatter.1
  440.3 61.0 all-gather.11
  504.6 59.1 all-gather.13
  567.1 59.1 all-gather.15
  629.6 59.1 all-gather.17
  690.4 18.6 all-gather.7
  711.8 61.5 all-gather.19
where the time goes:
time: 807 us; the launch traced here: 798 us
  waiting for transfers between devices  449 us (56%)
  other arithmetic  130 us (16%)
  local copies, waits for them, and re-layouts  76.3 us (9%)
  matrix products  66.5 us (8%)
  blocking collectives  42.7 us (5%)
  starting transfers between devices  18.8 us (2%)
  between operations  14.9 us (2%)
    all_gather x2, waiting for transfers between devices, on_device(): segment = lax.all_gather(correction, 'dom', axis=0, tiled=True)  116 us
    all_gather x2, waiting for transfers between devices, on_device(): lax.all_gather(current_y, 'dom', axis=0, tiled=True)  114 us
    scatter-add x3, other arithmetic, apply_hamiltonian(): assembled.at[connectivity.reshape(-1)].add(products.reshape(-1, band_width))  82.9 us
    reduce_scatter x1, waiting for transfers between devices, on_device(): lax.psum_scatter(partial_margin, 'dom', scatter_dimension=0, tiled=True)  82.7 us
    all_gather x1, waiting for transfers between devices, on_device(): root_columns = lax.all_gather(inverse_root, 'dom', axis=0, tiled=True)  64.4 us
    gather x3, local copies, waits for them, and re-layouts, apply_hamiltonian(): gathered = jnp.take(extended, connectivity, axis=0)  52 us
    psum x1, blocking collectives, on_device(): mean_eigen = lax.psum(trace_part, ('dom', 'band')) / STATES  37 us
    ppermute x6, waiting for transfers between devices, passed_along(): lax.ppermute(value, axis, [(source, source + steps) for source in range(i...  36 us
  transfers between devices with their start and end apart: 14, of which 14 were waited for; matrix products, arithmetic and copies ran while one was open for 2% of the time, Pallas kernels for 0%

commit v1 on v0

v1 whole, which is shorter than its diff:
```python
import functools

import jax
import jax.numpy as jnp
from jax import lax
from jax.experimental import pallas as pl
from jax.experimental.pallas import tpu as pltpu
from jax.sharding import PartitionSpec as P

filter_center = 5.0
filter_half = 5.0
MESH = pl.DeviceIdType.MESH
VMEM_LIMIT = 62 * 1024 * 1024


def row_tile(rows, most):
    return max(t for t in range(16, most + 1, 16) if rows % t == 0)


def dot32(a, b, dims=((1,), (0,))):
    return lax.dot_general(a, b, (dims, ((), ())), preferred_element_type=jnp.float32)


def operator_kernel(share, conn_ref, a_ref, m_ref, ht, b, send_sem, recv_sem):
    cells, nodes = conn_ref.shape
    extent, width = m_ref.shape[1], b.shape[1]
    me = lax.axis_index("band") if share > 1 else 0
    if share > 1:
        barrier = pltpu.get_barrier_semaphore()
        for step in range(1, share):
            peer = lax.rem(me + step, share)
            pl.semaphore_signal(barrier, inc=1, device_id={"band": peer}, device_id_type=MESH)
        pl.semaphore_wait(barrier, share - 1)
    build = row_tile(extent, 256)

    @pl.loop(0, cells)
    def _(c):
        links = conn_ref[pl.ds(c, 1), :]
        span = pl.ds(pl.multiple_of(c * nodes, 128), nodes)

        @pl.loop(0, extent // build)
        def _(r):
            ids = lax.broadcasted_iota(jnp.int32, (build, nodes), 0) + r * build
            ht[pl.ds(pl.multiple_of(r * build, build), build), span] = jnp.where(
                ids == links, 1.0, 0.0
            ).astype(jnp.bfloat16)

    first = pl.multiple_of(me * width, 128) if share > 1 else 0

    @pl.loop(0, cells)
    def _(c):
        span = pl.ds(pl.multiple_of(c * nodes, 128), nodes)
        picks = ht[pl.ds(first, width), span]
        b[span, :] = dot32(a_ref[c], picks, ((1,), (1,))).astype(jnp.bfloat16)

    tile = row_tile(extent, 384)
    tiles = extent // tile

    def copies(r):
        rows = pl.ds(pl.multiple_of(r * tile, tile), tile)
        return [
            pltpu.make_async_remote_copy(
                src_ref=m_ref.at[me, rows],
                dst_ref=m_ref.at[me, rows],
                send_sem=send_sem.at[step, r],
                recv_sem=recv_sem.at[step, r],
                device_id={"band": lax.rem(me + step, share)},
                device_id_type=MESH,
            )
            for step in range(1, share)
        ]

    @pl.loop(0, tiles)
    def _(r):
        rows = pl.ds(pl.multiple_of(r * tile, tile), tile)
        total = dot32(ht[rows, :], b[...])
        kept = total.astype(jnp.bfloat16)
        m_ref[me, rows, :width] = kept
        offsets = lax.broadcasted_iota(jnp.int32, (tile, width), 1) - lax.broadcasted_iota(
            jnp.int32, (tile, width), 0
        )
        rest = jnp.where(
            offsets == r * tile - me * width, total - kept.astype(jnp.float32), 0.0
        )
        rest = jnp.sum(rest, axis=1, keepdims=True)
        m_ref[me, rows, width:] = jnp.broadcast_to(rest, (tile, 128)).astype(jnp.bfloat16)
        for copy in copies(r):
            copy.start()

    @pl.loop(0, tiles)
    def _(r):
        for copy in copies(r):
            copy.wait()


def domain_operator(cell_matrices, connectivity, extent):
    cells, nodes = connectivity.shape
    share = lax.axis_size("band")
    if extent % (share * 128):
        share = 1
    width = extent // share
    tiles = extent // row_tile(extent, 384)
    vmem = pl.BlockSpec(memory_space=pltpu.VMEM)
    params = dict(collective_id=0, has_side_effects=True) if share > 1 else {}
    halves = pl.pallas_call(
        functools.partial(operator_kernel, share),
        out_shape=jax.ShapeDtypeStruct((share, extent, width + 128), jnp.bfloat16),
        in_specs=[vmem] * 2,
        out_specs=vmem,
        scratch_shapes=[
            pltpu.VMEM((extent, cells * nodes), jnp.bfloat16),
            pltpu.VMEM((cells * nodes, width), jnp.bfloat16),
            pltpu.SemaphoreType.DMA((share, tiles)),
            pltpu.SemaphoreType.DMA((share, tiles)),
        ],
        compiler_params=pltpu.CompilerParams(vmem_limit_bytes=VMEM_LIMIT, **params),
        name="domain_operator",
    )(connectivity, cell_matrices)
    rest = sum(halves[i, :, width:].astype(jnp.float32) for i in range(share))
    return jnp.concatenate([halves[i, :, :width] for i in range(share)], axis=1), rest


def passed_along(value, axis, steps):
    count = lax.axis_size(axis)
    initial, last = (max(0, -steps), min(count, count - steps))
    return lax.ppermute(value, axis, [(source, source + steps) for source in range(initial, last)])


def on_device(wavefunctions, mass_scale, cell_matrices, connectivity, face_index):
    bf16 = jnp.bfloat16
    own, band_width = wavefunctions.shape
    face = face_index.shape[0]
    domains = lax.axis_size("dom")
    states = band_width * lax.axis_size("band")
    matrix, rest = domain_operator(cell_matrices, connectivity, own + face)
    face_of = (face_index[:, None] == lax.broadcasted_iota(jnp.int32, (face, own), 1)).astype(bf16)
    face_in = (face_index[None, :] == lax.broadcasted_iota(jnp.int32, (own, face), 0)).astype(bf16)
    outgoing = jnp.concatenate([matrix[own:, :own], face_of], axis=0)
    inner = matrix[:own, :own]
    edge = jnp.concatenate([matrix[:own, own:], face_in, face_in], axis=1)
    corner = jnp.concatenate([matrix[own:, own:], rest[own:].astype(bf16)], axis=1)
    corner = passed_along(corner, "dom", 1)
    corner, corner_rest = corner[:, :face], corner[:, face : face + 1].astype(jnp.float32)
    rest = rest[:own, :1]
    mass = mass_scale[:, None]

    def hamiltonian(vectors):
        scaled = (mass * vectors).astype(bf16)
        sent = dot32(outgoing, scaled).astype(bf16)
        returned = passed_along(sent[:face], "dom", 1)
        received = passed_along(sent[face:], "dom", -1)
        summed = dot32(inner, scaled) + rest * scaled.astype(jnp.float32)
        added = returned.astype(jnp.float32) + dot32(corner, sent[face:])
        added = added + corner_rest * sent[face:].astype(jnp.float32)
        high = added.astype(bf16)
        low = (added - lax.reduce_precision(added, 8, 7)).astype(bf16)
        summed = summed + dot32(edge, jnp.concatenate([received, high, low], axis=0))
        return mass * summed

    previous = wavefunctions.astype(jnp.float32)
    current = (hamiltonian(previous) - filter_center * previous) / filter_half
    for _ in range(2):
        following = 2.0 * (hamiltonian(current) - filter_center * current) / filter_half - previous
        previous, current = (current, following)
    rounded = current.astype(bf16)
    everyone = lax.all_gather(rounded, "band", axis=1, tiled=True)
    partial = dot32(everyone, rounded, ((0,), (0,))) / (own * domains)
    tile = lax.psum_scatter(partial.astype(bf16), "dom", scatter_dimension=0, tiled=True)
    columns = lax.all_gather(tile, "dom", axis=0, tiled=True)
    margin = lax.all_gather(columns, "band", axis=1, tiled=True).astype(jnp.float32)
    identity = (
        lax.broadcasted_iota(jnp.int32, (states, states), 0)
        == lax.broadcasted_iota(jnp.int32, (states, states), 1)
    ).astype(jnp.float32)
    mean_eigen = jnp.sum(margin * identity) / states
    offset = (margin / mean_eigen - identity).astype(bf16)
    start = lax.axis_index("band") * band_width
    first = lax.dynamic_slice_in_dim(columns.astype(jnp.float32), 0, states, 0) / mean_eigen
    first = first - lax.dynamic_slice_in_dim(identity, start, band_width, 1)
    second = dot32(offset, first.astype(bf16))
    third = dot32(offset, second.astype(bf16))
    tail = dot32(offset, (third / 16.0 - second * (5.0 / 16.0)).astype(bf16))
    change = tail + 0.375 * second - 0.5 * first
    turned = current + dot32(everyone, change.astype(bf16))
    return turned / jnp.sqrt(mean_eigen)


def solution(mesh):
    return jax.shard_map(
        on_device,
        mesh=mesh,
        in_specs=(P("dom", "band"), P("dom"), P("dom", None, None), P("dom", None), P("dom")),
        out_specs=P("dom", "band"),
        check_vma=False,
    )
```

time: 807 us -> 338 us (0.42)
  waiting for transfers between devices: 449 us -> 168 us
  other arithmetic: 130 us -> 11.3 us
  local copies, waits for them, and re-layouts: 76.3 us -> 10.8 us
  Pallas kernels: 0 us -> 47.1 us
  blocking collectives: 42.7 us -> 0 us
  matrix products: 66.5 us -> 56.1 us
    all_gather x7 -> x3, waiting for transfers between devices: 329 us -> 76.5 us  [the longest x1 53.9 us: on_device(): columns = lax.all_gather(tile, 'dom', axis=0, tiled=True)]
    scatter-add x6 -> x0, other arithmetic: 101 us -> none  [the longest x3 82.9 us: apply_hamiltonian(): assembled.at[connectivity.reshape(-1)].add(products.reshape(-1, band_width))]
    gather x6 -> x0, local copies, waits for them, and re-layouts: 59.3 us -> none  [the longest x3 52 us: apply_hamiltonian(): gathered = jnp.take(extended, connectivity, axis=0)]
    pallas_call x0 -> x1, Pallas kernels: none -> 47.1 us  [domain_operator(): pl.pallas_call(functools.partial(operator_kernel, share), out_shape=jax.S...]
    psum x1 -> x0, blocking collectives: 37 us -> none  [on_device(): mean_eigen = lax.psum(trace_part, ('dom', 'band')) / STATES]
    ppermute x6 -> x7, waiting for transfers between devices: 36 us -> 11.4 us  [passed_along(): lax.ppermute(value, axis, [(source, source + steps) for source in range(i...]
    convert_element_type x6 -> x3, other arithmetic: 19.9 us -> 3.28 us  [the longest x1 2.54 us: on_device(): identity = (lax.broadcasted_iota(jnp.int32, (states, states), 0) == lax.b...]
    slice x6, local copies, waits for them, and re-layouts: 17 us -> 1.43 us  [the longest x1 0.91 us: on_device(): matrix[own:, own:]]
  transfers between devices with their start and end apart: 14 -> 11, of which waited for: 14 -> 7; matrix products, arithmetic and copies ran while one was open for 2% -> 7% of each run, Pallas kernels for 0% -> 0%
where the time goes in v1:
time: 338 us; the launch traced here: 332 us
  waiting for transfers between devices  168 us (50%)
  matrix products  56.1 us (17%)
  Pallas kernels  47.1 us (14%)
  starting transfers between devices  24.7 us (7%)
  between operations  14.5 us (4%)
  other arithmetic  11.3 us (3%)
  local copies, waits for them, and re-layouts  10.8 us (3%)
    reduce_scatter x1, waiting for transfers between devices, on_device(): lax.psum_scatter(partial.astype(bf16), 'dom', scatter_dimension=0, tiled=...  80 us
    dot_general x16, matrix products, dot32(): lax.dot_general(a, b, (dims, ((), ())), preferred_element_type=jnp.float32)  56.1 us
    all_gather x1, waiting for transfers between devices, on_device(): columns = lax.all_gather(tile, 'dom', axis=0, tiled=True)  53.9 us
    pallas_call x1, Pallas kernels, domain_operator(): pl.pallas_call(functools.partial(operator_kernel, share), out_shape=jax.S...  47.1 us
    ppermute x7, starting transfers between devices, passed_along(): lax.ppermute(value, axis, [(source, source + steps) for source in range(i...  24.3 us
    all_gather x1, waiting for transfers between devices, on_device(): everyone = lax.all_gather(rounded, 'band', axis=1, tiled=True)  14.4 us
    ppermute x7, waiting for transfers between devices, passed_along(): lax.ppermute(value, axis, [(source, source + steps) for source in range(i...  11.4 us
    squeeze x1, local copies, waits for them, and re-layouts, domain_operator(): halves[i, :, :width]  8.85 us
  transfers between devices with their start and end apart: 11, of which 7 were waited for; matrix products, arithmetic and copies ran while one was open for 7% of the time, Pallas kernels for 0%

profile of v1, /device:TPU:0, one launch (start us, length us, event | category | flops | bytes accessed | tf_op | source)
XLA Modules:
  0.0 332.4 jit_solution(7075075881628874042)
XLA Ops:
  6.5 47.1 %domain_operator.1 = bf16[2,2304,1280]{2,1,0:T(8,128)(2,1)} custom-call(s32[8,512]{1,0:T(8,128)} %conn_ref.1, bf16[8,512,512]{2,1,0:T(8,128)(2,1)} %a_ref.1), custom_call_target="tpu_custom_call" | custom-call | tf_op jit(solution)/shard_map/domain_operator/pallas_call | solution.py:105
  53.7 1.4 convert_add_fusion
  55.1 8.8 %slice_bitcast_fusion = (bf16[2304,1152]{1,0:T(8,128)(2,1)}, bf16[2304,1152]{1,0:T(8,128)(2,1)}) fusion(bf16[2,2304,1280]{2,1,0:T(8,128)(2,1)} %domain_operator.1), kind=kLoop, calls=%fused_computation.6 | loop fusion | bytes 21233664 | tf_op jit(solution)/shard_map/squeeze | solution.py:120
  64.0 0.9 slice.86
  64.9 4.8 %collective-permute-start.2 = (bf16[256,384]{1,0:T(8,128)(2,1)S(1)}, bf16[256,384]{1,0:T(8,128)(2,1)S(1)}, u32[]{:S(2)}, u32[]{:S(2)}) collective-permute-start(bf16[256,384]{1,0:T(8,128)(2,1)S(1)} %pad_maximum_fusion.5), channel_id=1, source_target_pairs={{0,2},{2,4},{4,6},{6,8},{8,10},{10,12},{12,14},{14,16},{16,18},{18... | collective-permute-start | bytes 589832 | tf_op jit(solution)/shard_map/ppermute | solution.py:126
  69.7 0.2 fusion.9
  70.0 1.6 fusion.7
  71.6 0.4 copy-done.4
  72.0 1.4 convolution_convert_fusion.2
  73.4 1.4 collective-permute-start
  74.9 5.1 %collective-permute-start.1 = (bf16[256,512]{1,0:T(8,128)(2,1)S(1)}, bf16[256,512]{1,0:T(8,128)(2,1)S(1)}, u32[]{:S(2)}, u32[]{:S(2)}) collective-permute-start(bf16[256,512]{1,0:T(8,128)(2,1)S(1)} %get-tuple-element.16), channel_id=1, source_target_pairs={{0,2},{2,4},{4,6},{6,8},{8,10},{10,12},{12,14},{14,16},{16,18},{18... | collective-permute-start | bytes 786440 | tf_op jit(solution)/shard_map/ppermute | solution.py:126
  80.0 0.5 fusion.8
  80.5 1.4 fusion.58
  81.9 1.2 fusion
  83.1 4.8 %fusion.31 = f32[2048,512]{1,0:T(8,128)S(1)} fusion(bf16[2048,2048]{1,0:T(8,128)(2,1)S(1)} %fusion, bf16[2048,512]{1,0:T(8,128)(2,1)S(1)} %copy-done.4, f32[2048]{0:T(1024)S(1)} %copy-done.2), kind=kOutput, calls=%fused_computation.58 | convolution fusion | flops 4298113024 | bytes 14688256 | tf_op jit(solution)/shard_map/dot_general | solution.py:21
  87.9 0.1 slice.83
  88.0 0.3 slice_reduce_fusion
  88.3 0.1 convert_reduce_fusion
  88.4 1.6 collective-permute-done.1
  90.0 0.3 fusion.69
  90.3 2.6 fusion.5
  92.9 1.3 convolution_convert_fusion.1
  94.3 1.3 collective-permute-start.3
  95.6 5.2 %collective-permute-start.4 = (bf16[256,512]{1,0:T(8,128)(2,1)S(1)}, bf16[256,512]{1,0:T(8,128)(2,1)S(1)}, u32[]{:S(2)}, u32[]{:S(2)}) collective-permute-start(bf16[256,512]{1,0:T(8,128)(2,1)S(1)} %get-tuple-element.12), channel_id=1, source_target_pairs={{0,2},{2,4},{4,6},{6,8},{8,10},{10,12},{12,14},{14,16},{16,18},{18... | collective-permute-start | bytes 786440 | tf_op jit(solution)/shard_map/ppermute | solution.py:126
  100.7 4.8 %fusion.60 = f32[2048,512]{1,0:T(8,128)S(1)} fusion(bf16[2048,2048]{1,0:T(8,128)(2,1)S(1)} %fusion, f32[2048,512]{1,0:T(8,128)S(1)} %fusion.5, f32[2048]{0:T(1024)S(1)} %broadcast_multiply_fusion), kind=kOutput, calls=%fused_computation.87 | convolution fusion | flops 4297064448 | bytes 16785408 | tf_op jit(solution)/shard_map/dot_general | solution.py:21
  105.5 4.8 %collective-permute-done.4 = bf16[256,512]{1,0:T(8,128)(2,1)S(1)} collective-permute-done((bf16[256,512]{1,0:T(8,128)(2,1)S(1)}, bf16[256,512]{1,0:T(8,128)(2,1)S(1)}, u32[]{:S(2)}, u32[]{:S(2)}) %collective-permute-start.4) | collective-permute-done | bytes 262176 | tf_op jit(solution)/shard_map/ppermute | solution.py:126
  110.3 0.3 fusion.67
  110.6 3.1 convert_subtract_fusion
  113.7 1.4 convolution_convert_fusion
  115.2 1.3 collective-permute-start.5
  116.5 5.2 %collective-permute-start.6 = (bf16[256,512]{1,0:T(8,128)(2,1)S(1)}, bf16[256,512]{1,0:T(8,128)(2,1)S(1)}, u32[]{:S(2)}, u32[]{:S(2)}) collective-permute-start(bf16[256,512]{1,0:T(8,128)(2,1)S(1)} %get-tuple-element.8), channel_id=1, source_target_pairs={{0,2},{2,4},{4,6},{6,8},{8,10},{10,12},{12,14},{14,16},{16,18},{18... | collective-permute-start | bytes 786440 | tf_op jit(solution)/shard_map/ppermute | solution.py:126
  121.7 4.8 %fusion.59 = f32[2048,512]{1,0:T(8,128)S(1)} fusion(bf16[2048,2048]{1,0:T(8,128)(2,1)S(1)} %fusion, f32[2048,512]{1,0:T(8,128)S(1)} %convert_subtract_fusion, f32[2048]{0:T(1024)S(1)} %copy-done.2), kind=kOutput, calls=%fused_computation.86 | convolution fusion | flops 4297064448 | bytes 16785408 | tf_op jit(solution)/shard_map/dot_general | solution.py:21
  126.5 5.0 %collective-permute-done.6 = bf16[256,512]{1,0:T(8,128)(2,1)S(1)} collective-permute-done((bf16[256,512]{1,0:T(8,128)(2,1)S(1)}, bf16[256,512]{1,0:T(8,128)(2,1)S(1)}, u32[]{:S(2)}, u32[]{:S(2)}) %collective-permute-start.6) | collective-permute-done | bytes 262176 | tf_op jit(solution)/shard_map/ppermute | solution.py:126
  131.5 0.3 fusion.65
  131.8 4.7 %fusion.70 = (bf16[2048,512]{1,0:T(8,128)(2,1)}, f32[2048,512]{1,0:T(8,128)}) fusion(f32[2048,512]{1,0:T(8,128)S(1)} %fusion.5, f32[2048,512]{1,0:T(8,128)S(1)} %convert_subtract_fusion, bf16[256,512]{1,0:T(8,128)(2,1)S(1)} %get-tuple-element.10, bf16[256,512]{1,0:T(8,128)(2,1)S(1)} %get-tuple-element.9, bf16[256,512]{1,0:T(8,128)(2,1)S(1)} %collective-permute-done.5, ...), kind=kOutput, calls=%fused_computation.94 | convolution fusion | flops 1636040704 | bytes 21774336 | tf_op jit(solution)/shard_map/dot_general | solution.py:21
  136.5 0.0 reduce-scatter.2.cloned.1.call-start
  136.6 14.4 %all-gather.4.cloned.1.call-done = bf16[2048,1024]{1,0:T(8,128)(2,1)} async-done(((bf16[2048,512]{1,0:T(8,128)(2,1)}), bf16[2048,1024]{1,0:T(8,128)(2,1)}) %all-gather.4.cloned.1.call-update) | async-done | bytes 4194320 | tf_op jit(solution)/shard_map/all_gather | solution.py:166
  150.9 6.2 %multiply_convert_fusion.2 = bf16[1024,512]{1,0:T(8,128)(2,1)} fusion(bf16[2048,1024]{1,0:T(8,128)(2,1)} %all-gather.4.cloned.1.call-done, bf16[2048,512]{1,0:T(8,128)(2,1)} %get-tuple-element.19), kind=kOutput, calls=%fused_computation.27 | convolution fusion | flops 2148532224 | bytes 7340032 | tf_op jit(solution)/shard_map/dot_general | solution.py:21
  157.1 0.0 all-gather.6.cloned.1.call-start
  157.2 80.0 %reduce-scatter.2.cloned.1.call-done = bf16[64,512]{1,0:T(8,128)(2,1)} async-done(((bf16[1024,512]{1,0:T(8,128)(2,1)}), bf16[64,512]{1,0:T(8,128)(2,1)}) %reduce-scatter.2.cloned.1.call-update) | async-done | bytes 65552 | tf_op jit(solution)/shard_map/reduce_scatter | solution.py:168
  237.2 0.3 all-gather.8.cloned.1.call-start
  237.5 53.9 %all-gather.6.cloned.1.call-done = bf16[1024,512]{1,0:T(8,128)(2,1)} async-done(((bf16[64,512]{1,0:T(8,128)(2,1)}), bf16[1024,512]{1,0:T(8,128)(2,1)}) %all-gather.6.cloned.1.call-update) | async-done | bytes 1048592 | tf_op jit(solution)/shard_map/all_gather | solution.py:169
  291.5 2.5 fusion.6
  294.0 8.3 %all-gather.8.cloned.1.call-done = bf16[1024,1024]{1,0:T(8,128)(2,1)} async-done(((bf16[1024,512]{1,0:T(8,128)(2,1)}), bf16[1024,1024]{1,0:T(8,128)(2,1)}) %all-gather.8.cloned.1.call-update) | async-done | bytes 2097168 | tf_op jit(solution)/shard_map/all_gather | solution.py:170
  302.3 2.4 fusion.1
  305.3 5.0 %fusion.11 = f32[1024,512]{1,0:T(8,128)} fusion(f32[1024,1024]{1,0:T(8,128)} %fusion.6, s32[]{:T(128)S(6)} %select_n.3, bf16[1024,512]{1,0:T(8,128)(2,1)S(1)} %copy-done.1, f32[]{:T(128)S(6)} %div.50, bf16[1024,1024]{1,0:T(8,128)(2,1)} %all-gather.8.cloned.1.call-done), kind=kOutput, calls=%fused_computation.38 | convolution fusion | flops 1082130432 | bytes 7341568 | tf_op jit(solution)/shard_map/dot_general | solution.py:21
  310.4 7.1 %subtract_convert_fusion = bf16[1024,512]{1,0:T(8,128)(2,1)} fusion(f32[1024,512]{1,0:T(8,128)} %fusion.11, f32[1024,1024]{1,0:T(8,128)} %fusion.6, s32[]{:T(128)S(6)} %select_n.3, f32[]{:T(128)S(6)} %div.50, bf16[1024,512]{1,0:T(8,128)(2,1)S(1)} %copy-done.1, bf16[1024,1024]{1,0:T(8,128)(2,1)S(1)} %copy-done), kind=kOutput, calls=%fused_computation.24 | convolution fusion | flops 2166882304 | bytes 14682112 | tf_op jit(solution)/shard_map/dot_general | solution.py:21
  317.5 8.1 %add_divide_fusion = f32[2048,512]{1,0:T(8,128)} fusion(f32[2048,512]{1,0:T(8,128)} %get-tuple-element.20, bf16[2048,1024]{1,0:T(8,128)(2,1)} %all-gather.4.cloned.1.call-done, bf16[1024,512]{1,0:T(8,128)(2,1)} %subtract_convert_fusion, f32[]{:T(128)S(6)} %sqrt.3), kind=kOutput, calls=%fused_computation.15 | convolution fusion | flops 2149580800 | bytes 13631492 | tf_op jit(solution)/shard_map/dot_general | solution.py:21
  (34 shorter events, 0.3 us)
Async XLA Ops:
  6.5 144.4 %all-gather.4.cloned.1.call-start = ((), (), s32[]{:S(2)}) async-start(), calls=%async_computation.1 | async-start | bytes 6291456 | tf_op jit(solution)/shard_map/all_gather | solution.py:166
  55.1 14.6 %copy-start.3 = (s32[256]{0:T(256)S(1)}, s32[256]{0:T(256)}, u32[]{:S(2)}) copy-start(s32[256]{0:T(256)} %param.9) | copy-start | bytes 3076
  64.9 23.4 %collective-permute-start.2 = (bf16[256,384]{1,0:T(8,128)(2,1)S(1)}, bf16[256,384]{1,0:T(8,128)(2,1)S(1)}, u32[]{:S(2)}, u32[]{:S(2)}) collective-permute-start(bf16[256,384]{1,0:T(8,128)(2,1)S(1)} %pad_maximum_fusion.5), channel_id=1, source_target_pairs={{0,2},{2,4},{4,6},{6,8},{8,10},{10,12},{12,14},{14,16},{16,18},{18... | collective-permute-start | bytes 589832 | tf_op jit(solution)/shard_map/ppermute | solution.py:126
  69.9 11.9 %slice-start = ((s8[5308416]{0:T(1024)(128)(4,1)}), s8[4194304]{0:T(1024)(128)(4,1)S(1)}, s32[]{:S(2)}) async-start(s8[5308416]{0:T(1024)(128)(4,1)} %bitcast.18), calls=%async_computation.5 | async-start | bytes 8388608
  69.9 11.9 %slice-start.2 = ((s8[5308416]{0:T(1024)(128)(4,1)}), s8[4194304]{0:T(1024)(128)(4,1)S(1)}, s32[]{:S(2)}) async-start(s8[5308416]{0:T(1024)(128)(4,1)} %bitcast.20), calls=%async_computation.7 | async-start | bytes 8388608
  70.0 1.6 copy-start.2
  70.0 2.1 copy-start.4
  70.0 11.9 %slice-start.1 = ((s8[5308416]{0:T(1024)(128)(4,1)}), s8[1114112]{0:T(1024)(128)(4,1)S(1)}, s32[]{:S(2)}) async-start(s8[5308416]{0:T(1024)(128)(4,1)} %bitcast.18), calls=%async_computation.6 | async-start | bytes 2228224
  70.0 11.9 %slice-start.3 = ((s8[5308416]{0:T(1024)(128)(4,1)}), s8[1114112]{0:T(1024)(128)(4,1)S(1)}, s32[]{:S(2)}) async-start(s8[5308416]{0:T(1024)(128)(4,1)} %bitcast.20), calls=%async_computation.8 | async-start | bytes 2228224
  73.4 16.9 %collective-permute-start = (bf16[256,512]{1,0:T(8,128)(2,1)S(1)}, bf16[256,512]{1,0:T(8,128)(2,1)S(1)}, u32[]{:S(2)}, u32[]{:S(2)}) collective-permute-start(bf16[256,512]{1,0:T(8,128)(2,1)S(1)} %get-tuple-element.15), channel_id=1, source_target_pairs={{2,0},{4,2},{6,4},{8,6},{10,8},{12,10},{14,12},{16,14},{18,16},{20... | collective-permute-start | bytes 786440 | tf_op jit(solution)/shard_map/ppermute | solution.py:126
  74.9 15.1 %collective-permute-start.1 = (bf16[256,512]{1,0:T(8,128)(2,1)S(1)}, bf16[256,512]{1,0:T(8,128)(2,1)S(1)}, u32[]{:S(2)}, u32[]{:S(2)}) collective-permute-start(bf16[256,512]{1,0:T(8,128)(2,1)S(1)} %get-tuple-element.16), channel_id=1, source_target_pairs={{0,2},{2,4},{4,6},{6,8},{8,10},{10,12},{12,14},{14,16},{16,18},{18... | collective-permute-start | bytes 786440 | tf_op jit(solution)/shard_map/ppermute | solution.py:126
  94.3 16.4 %collective-permute-start.3 = (bf16[256,512]{1,0:T(8,128)(2,1)S(1)}, bf16[256,512]{1,0:T(8,128)(2,1)S(1)}, u32[]{:S(2)}, u32[]{:S(2)}) collective-permute-start(bf16[256,512]{1,0:T(8,128)(2,1)S(1)} %get-tuple-element.11), channel_id=1, source_target_pairs={{2,0},{4,2},{6,4},{8,6},{10,8},{12,10},{14,12},{16,14},{18,16},{20... | collective-permute-start | bytes 786440 | tf_op jit(solution)/shard_map/ppermute | solution.py:126
  95.6 14.8 %collective-permute-start.4 = (bf16[256,512]{1,0:T(8,128)(2,1)S(1)}, bf16[256,512]{1,0:T(8,128)(2,1)S(1)}, u32[]{:S(2)}, u32[]{:S(2)}) collective-permute-start(bf16[256,512]{1,0:T(8,128)(2,1)S(1)} %get-tuple-element.12), channel_id=1, source_target_pairs={{0,2},{2,4},{4,6},{6,8},{8,10},{10,12},{12,14},{14,16},{16,18},{18... | collective-permute-start | bytes 786440 | tf_op jit(solution)/shard_map/ppermute | solution.py:126
  115.2 16.6 %collective-permute-start.5 = (bf16[256,512]{1,0:T(8,128)(2,1)S(1)}, bf16[256,512]{1,0:T(8,128)(2,1)S(1)}, u32[]{:S(2)}, u32[]{:S(2)}) collective-permute-start(bf16[256,512]{1,0:T(8,128)(2,1)S(1)} %get-tuple-element.7), channel_id=1, source_target_pairs={{2,0},{4,2},{6,4},{8,6},{10,8},{12,10},{14,12},{16,14},{18,16},{20... | collective-permute-start | bytes 786440 | tf_op jit(solution)/shard_map/ppermute | solution.py:126
  116.5 15.0 %collective-permute-start.6 = (bf16[256,512]{1,0:T(8,128)(2,1)S(1)}, bf16[256,512]{1,0:T(8,128)(2,1)S(1)}, u32[]{:S(2)}, u32[]{:S(2)}) collective-permute-start(bf16[256,512]{1,0:T(8,128)(2,1)S(1)} %get-tuple-element.8), channel_id=1, source_target_pairs={{0,2},{2,4},{4,6},{6,8},{8,10},{10,12},{12,14},{14,16},{16,18},{18... | collective-permute-start | bytes 786440 | tf_op jit(solution)/shard_map/ppermute | solution.py:126
  136.5 100.7 %reduce-scatter.2.cloned.1.call-start = ((), (), s32[]{:S(2)}) async-start(), calls=%async_computation.2 | async-start | bytes 1114112 | tf_op jit(solution)/shard_map/reduce_scatter | solution.py:168
  157.1 134.3 %all-gather.6.cloned.1.call-start = ((), (), s32[]{:S(2)}) async-start(), calls=%async_computation.3 | async-start | bytes 1114112 | tf_op jit(solution)/shard_map/all_gather | solution.py:169
  237.2 65.0 %all-gather.8.cloned.1.call-start = ((), (), s32[]{:S(2)}) async-start(), calls=%async_computation.4 | async-start | bytes 3145728 | tf_op jit(solution)/shard_map/all_gather | solution.py:170
  291.4 13.9 %copy-start.1 = (bf16[1024,512]{1,0:T(8,128)(2,1)S(1)}, bf16[1024,512]{1,0:T(8,128)(2,1)}, u32[]{:S(2)}) copy-start(bf16[1024,512]{1,0:T(8,128)(2,1)} %all-gather.6.cloned.1.call-done) | copy-start | bytes 3145732
  305.3 5.0 %copy-start = (bf16[1024,1024]{1,0:T(8,128)(2,1)S(1)}, bf16[1024,1024]{1,0:T(8,128)(2,1)}, u32[]{:S(2)}) copy-start(bf16[1024,1024]{1,0:T(8,128)(2,1)} %all-gather.8.cloned.1.call-done) | copy-start | bytes 6291460
Sparse Core Ops, SparseCore 0:
  136.6 14.2 all-gather.3
  157.2 79.9 reduce-scatter.1
  240.0 51.3 all-gather.5
  292.8 9.3 all-gather.7
